TPU v7x, 768 devices: a whole 4x8x12 slice. The times are simulated.
768 devices in a mesh: wide: 32 (over x_lo, y, core), narrow: 24 (over x_hi, z).
Axes of the slice: x: 4 (x_hi: 2, x_lo: 2; x = x_hi * 2 + x_lo), y: 8, z: 12, core: 2. Of those that a mesh axis runs over, the one named last changes fastest.
Arguments:
- diag_blocks: float32 [32, 512, 512], P('wide'), as said below
- row_panel: bfloat16 [32, 6144, 512], P('wide', 'narrow'), may hold values from -6 to 6
- col_panel: bfloat16 [32, 6144, 512], P('wide', 'narrow'), may hold values from -6 to 6
- row_tiles: int32 [32, 24], P('wide'), may hold values from 0 to 31, as said below
- col_mask: int32 [32, 24], P('wide', 'narrow'), may hold values 0 or 1
- slot_tile: int32 [32], replicated, may hold values from 0 to 31, each once
- trailing: float32 [8192, 6144], P('wide', 'narrow'), may hold values from -6 to 6
Outputs:
- schur_block: float32 [8192, 6144], P('wide', 'narrow')
Inputs may be any that keep to these rules, and one draw needn't show every extreme that they name: `row_tiles`: the 24 ids of one supernode are distinct. `slot_tile`: a permutation of the row-tile ids. `diag_blocks`: each block is symmetric and positive definite, its smallest eigenvalue at least 30.
All inputs are finite; a program needn't handle non-finite values. No bound on the sum of `col_mask` on one device may be relied on, other than what follows from the above.
Results may differ from a plain program's by a relative error of at most 0.013.
Values may be sent and summed in bfloat16 or wider, within the bound.
No kernel may reach another device: no remote copies, remote signals or barrier semaphores. Data moves between devices by JAX's collectives and lax.ppermute only.
A program may use at most 64 MiB of HBM per device.

v0:
```python
import jax
import jax.numpy as jnp
from jax import lax
from jax.sharding import PartitionSpec as P


def solve_single(panel, factor_low):
    solved = lax.linalg.triangular_solve(
        factor_low, panel.astype(jnp.float32), left_side=False, lower=True, transpose_a=True
    )
    return solved.astype(jnp.bfloat16)


def solve_rows(panel, factor_low):
    return jax.vmap(solve_single)(panel, factor_low)


def local(diag_blocks, row_panel, col_panel, row_tiles, col_mask, slot_tile, trailing):
    tile_rows = col_panel.shape[1]
    slot_count = slot_tile.shape[0]
    factor_low = jax.vmap(jnp.linalg.cholesky)(diag_blocks)
    col_factor = solve_rows(col_panel, factor_low)
    positions = jnp.arange(slot_count, dtype=jnp.int32)
    perm_table = (slot_tile[None, :] == positions[:, None]).astype(jnp.float32)
    tile_onehot = (row_tiles[:, :, None] == positions[None, None, :]).astype(jnp.float32)
    placing = jnp.einsum("sai,ip->sap", tile_onehot, perm_table, precision=lax.Precision.HIGHEST)
    placing = placing * col_mask.astype(jnp.float32)[:, :, None]
    row_factor = solve_rows(row_panel, factor_low)
    products = jnp.einsum(
        "sra,sca->src",
        lax.all_gather(row_factor, "narrow", axis=1, tiled=True),
        col_factor,
        preferred_element_type=jnp.float32,
    )
    supernodes = products.shape[0]
    blocks = products.reshape(supernodes, products.shape[1] // tile_rows, tile_rows, tile_rows)
    gathered_sum = jnp.einsum("sap,saij->pij", placing, blocks, precision=lax.Precision.HIGHEST)
    summed = lax.psum_scatter(
        gathered_sum.reshape(slot_count * tile_rows, tile_rows).astype(jnp.bfloat16),
        "wide",
        scatter_dimension=0,
        tiled=True,
    ).astype(jnp.float32)
    return trailing - summed


def solution(mesh):
    placed = (
        P("wide", None, None),
        P("wide", "narrow", None),
        P("wide", "narrow", None),
        P("wide", None),
        P("wide", "narrow"),
        P(),
        P("wide", "narrow"),
    )
    return jax.shard_map(
        local, mesh=mesh, in_specs=placed, out_specs=P("wide", "narrow"), check_vma=False
    )
```

profile of v0, /device:TPU:64, one launch (start us, length us, event | category | flops | bytes accessed | tf_op | source)
XLA Modules:
  0.0 482.2 jit_solution(5972792874606777556)
XLA Ops:
  6.5 1.6 copy.9
  8.1 1.4 fusion.18
  9.6 11.7 %custom-call.34 = f32[1,128,128]{2,1,0:T(8,128)S(1)} custom-call(f32[1,128,128]{2,1,0:T(8,128)S(1)} %cholesky.267), custom_call_target="Cholesky" | custom-call | tf_op jit(solution)/shard_map/vmap(jit(cholesky))/cholesky | solution.py:21
  21.4 9.8 %custom-call.35 = f32[1,1,128,128]{2,3,1,0:T(8,128)S(1)} custom-call(f32[1,1,128,128]{3,2,1,0:T(8,128)S(1)} %get-tuple-element.41), custom_call_target="InvertDiagBlocksLowerTriangular" | custom-call | tf_op jit(solution)/shard_map/vmap(jit(cholesky))/cholesky | solution.py:21
  31.2 0.1 cholesky.225
  31.3 0.0 copy-start.3
  31.3 0.3 constant_dynamic-update-slice_fusion.3
  31.7 0.3 fusion
  32.0 11.7 %custom-call.36 = f32[1,128,128]{2,1,0:T(8,128)S(1)} custom-call(f32[1,128,128]{2,1,0:T(8,128)S(1)} %cholesky.271), custom_call_target="Cholesky" | custom-call | tf_op jit(solution)/shard_map/vmap(jit(cholesky))/cholesky | solution.py:21
  43.8 10.2 %custom-call.37 = f32[1,1,128,128]{2,3,1,0:T(8,128)S(1)} custom-call(f32[1,1,128,128]{3,2,1,0:T(8,128)S(1)} %get-tuple-element.38), custom_call_target="InvertDiagBlocksLowerTriangular" | custom-call | tf_op jit(solution)/shard_map/vmap(jit(cholesky))/cholesky | solution.py:21
  54.0 0.3 fusion.1
  54.3 0.4 fusion.6
  54.7 11.7 %custom-call.38 = f32[1,128,128]{2,1,0:T(8,128)S(1)} custom-call(f32[1,128,128]{2,1,0:T(8,128)S(1)} %cholesky.276), custom_call_target="Cholesky" | custom-call | tf_op jit(solution)/shard_map/vmap(jit(cholesky))/cholesky | solution.py:21
  66.4 0.7 compare_reduce_fusion.1
  67.2 9.8 %custom-call.39 = f32[1,1,128,128]{2,3,1,0:T(8,128)S(1)} custom-call(f32[1,1,128,128]{3,2,1,0:T(8,128)S(1)} %get-tuple-element.35), custom_call_target="InvertDiagBlocksLowerTriangular" | custom-call | tf_op jit(solution)/shard_map/vmap(jit(cholesky))/cholesky | solution.py:21
  77.0 0.2 fusion.15
  77.2 0.4 fusion.16
  77.6 11.7 %custom-call.40 = f32[1,128,128]{2,1,0:T(8,128)S(1)} custom-call(f32[1,128,128]{2,1,0:T(8,128)S(1)} %fusion.16), custom_call_target="Cholesky" | custom-call | tf_op jit(solution)/shard_map/vmap(jit(cholesky))/cholesky | solution.py:21
  89.3 0.6 compare_reduce_fusion
  90.0 0.7 compare_reduce_fusion.2
  93.2 0.3 select_select_fusion
  93.5 8.1 %while.4 = (s32[]{:T(128)}, f32[1,512,512]{2,1,0:T(8,128)S(1)}, s32[4,2]{0,1:T(2,128)S(1)}, f32[4,1,128,128]{3,2,1,0:T(8,128)S(1)}, s32[]{:T(128)}) while((s32[]{:T(128)}, f32[1,512,512]{2,1,0:T(8,128)S(1)}, s32[4,2]{0,1:T(2,128)S(1)}, f32[4,1,128,128]{3,2,1,0:T(8,128)S(1)}, s32[]{:T(128)}) %tuple.32), condition=%wide.while_cond, body=%wide.while_body.sunk | while | flops 2 | bytes 131181 | solution.py:8
  93.5 0.1 constant_dynamic-slice_fusion.2
  93.6 0.6 fusion.61
  94.2 1.3 bitcast_dynamic-update-slice_fusion.2
  95.5 0.1 constant_dynamic-slice_fusion.2
  95.6 0.6 fusion.61
  96.2 1.3 bitcast_dynamic-update-slice_fusion.2
  97.6 0.1 constant_dynamic-slice_fusion.2
  97.7 0.6 fusion.61
  98.3 1.3 bitcast_dynamic-update-slice_fusion.2
  99.6 0.1 constant_dynamic-slice_fusion.2
  99.7 0.6 fusion.61
  100.3 1.3 bitcast_dynamic-update-slice_fusion.2
  101.6 39.3 %custom-call.42 = f32[1,4,128,128]{2,3,1,0:T(8,128)S(1)} custom-call(f32[1,4,128,128]{3,2,1,0:T(8,128)S(1)} %bitcast.236), custom_call_target="InvertDiagBlocksLowerTriangular" | custom-call | tf_op jit(solution)/shard_map/vmap()/triangular_solve/custom-call.3 | solution.py:8
  141.0 0.1 convert_element_type.27
  141.0 0.3 fusion.36
  141.4 0.4 fusion.3
  141.8 0.3 convolution_bitcast_fusion.12
  142.1 0.6 fusion.8
  142.7 0.3 convolution_bitcast_fusion.11
  143.0 0.8 fusion.12
  143.8 0.3 convolution_bitcast_fusion.10
  144.2 0.7 maximum_convert_fusion
  144.9 0.0 all-gather.2.cloned.1.call-update
  144.9 0.0 reduce-scatter.2.cloned.1.call-start
  145.0 0.1 convert_element_type.29
  145.7 0.2 fusion.17
  145.9 0.3 fusion.35
  146.2 0.4 fusion.5
  146.6 0.3 convolution_bitcast_fusion.8
  146.9 0.6 fusion.10
  147.5 0.3 convolution_bitcast_fusion.7
  147.8 0.8 fusion.14
  148.7 0.3 convolution_bitcast_fusion.6
  149.0 166.3 %all-gather.2.cloned.1.call-done = bf16[1,6144,512]{1,2,0:T(8,128)(2,1)} async-done(((bf16[1,256,512]{1,2,0:T(8,128)(2,1)}), bf16[1,6144,512]{1,2,0:T(8,128)(2,1)}) %all-gather.2.cloned.1.call-update) | async-done | bytes 6291472 | tf_op jit(solution)/shard_map/all_gather | solution.py:31
  315.3 7.6 %copy.12 = bf16[64,8,24,256]{3,2,1,0:T(8,128)(2,1)} copy(bf16[64,8,24,256]{3,1,2,0:T(8,128)(2,1)} %bitcast.228) | data formatting | bytes 12582912
  322.9 9.8 %copy.11 = bf16[24,256,512]{2,0,1:T(8,128)(2,1)} copy(bf16[24,256,512]{1,0,2:T(8,128)(2,1)} %bitcast.226) | data formatting | bytes 12582912 | tf_op jit(solution)/shard_map/reshape.144
  332.7 4.6 fusion.28
  337.3 7.1 %convolution_convert_fusion = bf16[32,256,256]{2,0,1:T(8,128)(2,1)S(1)} fusion(f32[24,32,1]{1,0,2:T(8,128)S(1)} %fusion.17, f32[24,256,256]{2,0,1:T(8,128)S(1)} %fusion.28), kind=kOutput, calls=%fused_computation.2 | convolution fusion | flops 606076928 | bytes 10488832 | tf_op jit(solution)/shard_map/sap,saij->pij/dot_general | solution.py:37
  344.4 4.3 copy.10
  348.7 0.0 reduce-scatter.2.cloned.1.call-update
  348.8 124.8 %reduce-scatter.2.cloned.1.call-done = bf16[256,256]{1,0:T(8,128)(2,1)} async-done(((bf16[8192,256]{1,0:T(8,128)(2,1)}), bf16[256,256]{1,0:T(8,128)(2,1)}) %reduce-scatter.2.cloned.1.call-update) | async-done | bytes 131088 | tf_op jit(solution)/shard_map/reduce_scatter | solution.py:38
  473.5 1.6 convert_subtract_fusion
  (20 shorter events, 0.2 us)
Async XLA Ops:
  6.5 308.8 %all-gather.2.cloned.1.call-start = ((), (), s32[]{:S(2)}) async-start(), calls=%async_computation.1 | async-start | bytes 6553600 | tf_op jit(solution)/shard_map/all_gather | solution.py:31
  6.5 134.4 %copy-start = (bf16[1,256,512]{2,1,0:T(8,128)(2,1)S(1)}, bf16[1,256,512]{2,1,0:T(8,128)(2,1)}, u32[]{:S(2)}) copy-start(bf16[1,256,512]{2,1,0:T(8,128)(2,1)} %param.10) | copy-start | bytes 786436
  31.2 113.8 %copy-start.1 = (bf16[1,256,512]{2,1,0:T(8,128)(2,1)S(1)}, bf16[1,256,512]{2,1,0:T(8,128)(2,1)}, u32[]{:S(2)}) copy-start(bf16[1,256,512]{2,1,0:T(8,128)(2,1)} %param.11) | copy-start | bytes 786436
  31.3 114.4 %copy-start.3 = (s32[32]{0:T(128)S(1)}, s32[32]{0:T(128)}, u32[]{:S(2)}) copy-start(s32[32]{0:T(128)} %param.14) | copy-start | bytes 388
  31.3 114.4 %copy-start.4 = (s32[1,24]{1,0:T(1,128)S(1)}, s32[1,24]{1,0:T(1,128)}, u32[]{:S(2)}) copy-start(s32[1,24]{1,0:T(1,128)} %param.12) | copy-start | bytes 292
  144.9 328.6 %reduce-scatter.2.cloned.1.call-start = ((), (), s32[]{:S(2)}) async-start(), calls=%async_computation.2 | async-start | bytes 4325376 | tf_op jit(solution)/shard_map/reduce_scatter | solution.py:38
  344.4 129.1 %copy-start.2 = (f32[256,256]{1,0:T(8,128)S(1)}, f32[256,256]{1,0:T(8,128)}, u32[]{:S(2)}) copy-start(f32[256,256]{1,0:T(8,128)} %param.15) | copy-start | bytes 786436
Sparse Core Ops, SparseCore 0:
  145.0 170.2 all-gather.1
  348.9 124.5 reduce-scatter.1
where the time goes:
time: 491 us; the launch traced here: 482 us
  waiting for transfers between devices  291 us (59%)
  other arithmetic  122 us (25%)
  local copies, waits for them, and re-layouts  31.5 us (6%)
  matrix products  19.9 us (4%)
  between operations  17.1 us (3%)
    all_gather x1, waiting for transfers between devices, local(): lax.all_gather(row_factor, 'narrow', axis=1, tiled=True)  166 us
    reduce_scatter x1, waiting for transfers between devices, local(): lax.psum_scatter(gathered_sum.reshape(slot_count * tile_rows, tile_rows)....  125 us
    another operation x14, other arithmetic, local(): factor_low = jax.vmap(jnp.linalg.cholesky)(diag_blocks)  78.9 us
    another operation x4, other arithmetic, solve_single(): lax.linalg.triangular_solve(factor_low, panel.astype(jnp.float32), left_s...  39.6 us
  transfers between devices with their start and end apart: 2, of which 2 were waited for; matrix products, arithmetic and copies ran while one was open for 1% of the time, Pallas kernels for 0%

commit v1 on v0

v1 whole, which is shorter than its diff:
```python
import jax
import jax.numpy as jnp
from jax import lax
from jax.experimental import pallas as pl
from jax.experimental.pallas import tpu as pltpu
from jax.sharding import Mesh, PartitionSpec as P

BLOCK = 128
GROUP = 8

def invert_block(block):
    size = block.shape[0]
    lanes = lax.broadcasted_iota(jnp.int32, (1, size), 1)
    for j in range(0, size, GROUP):
        columns = [
            jnp.broadcast_to(block[:, j + k : j + k + 1], (size, size)) for k in range(GROUP)
        ]
        pivots = [
            [columns[b][j + a : j + a + 1, :] if b >= a else None for b in range(GROUP)]
            for a in range(GROUP)
        ]
        rows = []
        for a in range(GROUP):
            inside = (lanes >= j) & (lanes < j + GROUP)
            unit = jnp.where(lanes == j + a, 1.0, 0.0)
            rows.append(jnp.where(inside, unit, block[j + a : j + a + 1, :]))
        factors = [None] * GROUP
        for k in range(GROUP):
            scale = 1.0 / pivots[k][k]
            factors[k] = {}
            for a in range(k + 1, GROUP):
                factor = pivots[k][a] * scale
                factors[k][a] = factor
                rows[a] = rows[a] - factor * rows[k]
                for b in range(a, GROUP):
                    pivots[a][b] = pivots[a][b] - factor * pivots[k][b]
            pivots[k][k] = scale
        for k in reversed(range(GROUP)):
            solved = rows[k] * pivots[k][k]
            for a in range(k + 1, GROUP):
                solved = solved - factors[k][a] * rows[a]
            rows[k] = solved
        outside = (lanes < j) | (lanes >= j + GROUP)
        rest = jnp.where(outside, block, 0.0)
        for k in range(GROUP):
            rest = rest - columns[k] * rows[k]
        parts = []
        if j > 0:
            parts.append(rest[:j])
        parts.append(jnp.concatenate(rows, axis=0))
        if j + GROUP < size:
            parts.append(rest[j + GROUP :])
        block = jnp.concatenate(parts, axis=0)
    return block


def exact_dot(left, right):
    return jnp.dot(left, right, precision=lax.Precision.HIGHEST, preferred_element_type=jnp.float32)


def solve_kernel(diag_ref, panel_ref, out_ref, work_ref, rhs_ref):
    width = diag_ref.shape[0]
    tile = panel_ref.shape[0]
    work_ref[...] = diag_ref[...]
    rhs_ref[...] = panel_ref[...].astype(jnp.float32).T
    steps = width // BLOCK
    for k in range(steps):
        here = slice(k * BLOCK, (k + 1) * BLOCK)
        inverse = invert_block(work_ref[here, here])
        solved = exact_dot(inverse, rhs_ref[here, :])
        rhs_ref[here, :] = solved
        last = (k + 1) * BLOCK
        if last < width:
            rest = exact_dot(inverse, work_ref[here, last:])
            work_ref[here, last:] = rest
        for i in range(steps):
            if i == k:
                continue
            there = slice(i * BLOCK, (i + 1) * BLOCK)
            multiplier = work_ref[there, here]
            rhs_ref[there, :] = rhs_ref[there, :] - exact_dot(multiplier, solved)
            if last < width:
                work_ref[there, last:] = work_ref[there, last:] - exact_dot(multiplier, rest)
    solved = rhs_ref[...]
    high = solved.astype(jnp.bfloat16)
    low = (solved - high.astype(jnp.float32)).astype(jnp.bfloat16)
    out_ref[:, :tile] = high
    out_ref[:, tile:] = low


def solve_panel(diag, panel):
    width, tile = diag.shape[0], panel.shape[0]
    return pl.pallas_call(
        solve_kernel,
        out_shape=jax.ShapeDtypeStruct((width, 2 * tile), jnp.bfloat16),
        scratch_shapes=[
            pltpu.VMEM((width, width), jnp.float32),
            pltpu.VMEM((width, tile), jnp.float32),
        ],
        name="solve_panel",
    )(diag, panel)


def product_kernel(table_ref, tile_ref, solved_ref, *rest):
    out_ref = rest[-1]
    step = pl.program_id(0)
    present = table_ref[step] >= 0
    width = out_ref.shape[1]

    @pl.when(present)
    def _():
        both = jnp.dot(tile_ref[...], solved_ref[...], preferred_element_type=jnp.float32)
        value = both[:, :width] + both[:, width:]
        if len(rest) == 2:
            value = value + rest[0][...].astype(jnp.float32)
        out_ref[...] = value.astype(out_ref.dtype)

    @pl.when(jnp.logical_not(present))
    def _():
        if len(rest) == 2:
            out_ref[...] = rest[0][...]
        else:
            out_ref[...] = jnp.zeros_like(out_ref)


def placed_products(table, tiles, solved, received, name):
    slots, width = table.shape[0], tiles.shape[1]
    tile = solved.shape[1] // 2
    by_slot = pl.BlockSpec((tile, tile), lambda i, table: (i, 0))
    in_specs = [
        pl.BlockSpec((tile, width), lambda i, table: (jnp.maximum(table[i], 0), 0)),
        pl.BlockSpec((width, 2 * tile), lambda i, table: (0, 0)),
    ]
    operands = [table, tiles, solved]
    if received is not None:
        in_specs.append(by_slot)
        operands.append(received)
    return pl.pallas_call(
        product_kernel,
        grid_spec=pltpu.PrefetchScalarGridSpec(
            num_scalar_prefetch=1, grid=(slots,), in_specs=in_specs, out_specs=by_slot
        ),
        out_shape=jax.ShapeDtypeStruct((slots * tile, tile), jnp.bfloat16),
        name=name,
    )(*operands)


def local(diag_blocks, row_panel, col_panel, row_tiles, col_mask, slot_tile, trailing):
    tile = trailing.shape[0]
    pair = lax.all_gather(row_panel[0], "x_hi", axis=0, tiled=True)
    tiles = lax.all_gather(pair, "z", axis=0, tiled=True)
    solved = solve_panel(diag_blocks[0], col_panel[0])

    count = row_tiles.shape[1]
    halves = lax.axis_size("x_hi")
    order = jnp.arange(count, dtype=jnp.int32)
    place = (order % (count // halves)) * halves + order // (count // halves)
    match = slot_tile[:, None] == row_tiles[0][None, :]
    table = jnp.max(jnp.where(match & (col_mask[0, 0] != 0), place[None, :], -1), axis=1)
    table = table.reshape(-1, 2)
    core = lax.axis_index("core")
    mine = jnp.where(core == 0, table[:, 0], table[:, 1])
    other = jnp.where(core == 0, table[:, 1], table[:, 0])

    sent = placed_products(other, tiles, solved, None, "products_sent")
    received = lax.ppermute(sent, "core", [(0, 1), (1, 0)])
    partial = placed_products(mine, tiles, solved, received, "products_kept")
    pieces = lax.all_to_all(partial, ("x_lo", "y"), 0, 0, tiled=True)
    pieces = pieces.reshape(-1, tile, tile).astype(jnp.float32)
    return trailing - jnp.sum(pieces, axis=0)


def solution(mesh):
    wide, narrow = mesh.shape["wide"], mesh.shape["narrow"]
    split = Mesh(
        mesh.devices.reshape(2, wide // 4, 2, 2, narrow // 2), ("x_lo", "y", "core", "x_hi", "z")
    )
    w, n = ("x_lo", "y", "core"), ("x_hi", "z")
    placed = (P(w), P(w, n), P(w, n), P(w), P(w, n), P(), P(w, n))
    return jax.shard_map(local, mesh=split, in_specs=placed, out_specs=P(w, n), check_vma=False)
```

time: 491 us -> 207 us (0.42)
  the two profiles are of different devices: /device:TPU:64 before, /device:TPU:14 now
where the time goes in v1:
time: 207 us; the launch traced here: 206 us
  blocking collectives  74.1 us (36%)
  waiting for transfers between devices  67.4 us (33%)
  Pallas kernels  43.4 us (21%)
  between operations  14.1 us (7%)
  other arithmetic  2.49 us (1%)
  local copies, waits for them, and re-layouts  2.09 us (1%)
    all_to_all x1, blocking collectives, local(): pieces = lax.all_to_all(partial, ('x_lo', 'y'), 0, 0, tiled=True)  63.6 us
    all_gather x1, waiting for transfers between devices, local(): tiles = lax.all_gather(pair, 'z', axis=0, tiled=True)  63 us
    pallas_call x1, Pallas kernels, solve_panel(): pl.pallas_call(solve_kernel, out_shape=jax.ShapeDtypeStruct((width, 2 * t...  25.9 us
    pallas_call x2, Pallas kernels, placed_products(): pl.pallas_call(product_kernel, grid_spec=pltpu.PrefetchScalarGridSpec(num...  17.5 us
    all_gather x1, blocking collectives, local(): pair = lax.all_gather(row_panel[0], 'x_hi', axis=0, tiled=True)  10.5 us
    ppermute x1, waiting for transfers between devices, local(): received = lax.ppermute(sent, 'core', [(0, 1), (1, 0)])  4.34 us
  transfers between devices with their start and end apart: 2, of which 2 were waited for; matrix products, arithmetic and copies ran while one was open for 1% of the time, Pallas kernels for 13%

profile of v1, /device:TPU:14, one launch (start us, length us, event | category | flops | bytes accessed | tf_op | source)
XLA Modules:
  0.0 205.5 jit_solution(18051601511148067016)
XLA Ops:
  6.5 0.0 all-gather.4.cloned.1.call-start
  6.5 10.5 %all-gather = bf16[1,512,512]{2,1,0:T(8,128)(2,1)} all-gather(bf16[1,256,512]{2,1,0:T(8,128)(2,1)} %param.8), channel_id=2, replica_groups=mesh['x_lo'=2,'y'=8,'core'=2,'x_hi'=2,'z'=12] {'x_hi'}, dimensions={1}, use_global_device_ids=true | all-gather | bytes 786432 | tf_op jit(solution)/shard_map/all_gather | solution.py:150
  17.1 0.0 all-gather.4.cloned.1.call-update
  17.8 0.8 select_reduce_fusion
  18.5 0.1 reshape.33
  18.6 25.9 %solve_panel.1.solved_ref = bf16[512,512]{1,0:T(8,128)(2,1)} custom-call(f32[512,512]{1,0:T(8,128)} %bitcast.9, bf16[256,512]{1,0:T(8,128)(2,1)} %bitcast.10), custom_call_target="tpu_custom_call" | custom-call | tf_op jit(solution)/shard_map/solve_panel/pallas_call | solution.py:93
  44.5 0.7 select_reduce_fusion.1
  45.2 63.0 %all-gather.4.cloned.1.call-done = bf16[1,6144,512]{2,1,0:T(8,128)(2,1)} async-done(((bf16[1,512,512]{2,1,0:T(8,128)(2,1)}), bf16[1,6144,512]{2,1,0:T(8,128)(2,1)}) %all-gather.4.cloned.1.call-update) | async-done | bytes 6291472 | tf_op jit(solution)/shard_map/all_gather | solution.py:151
  108.2 7.1 %products_sent.1 = bf16[4096,256]{1,0:T(8,128)(2,1)} custom-call(s32[16]{0:T(128)} %get-tuple-element.5.table_ref, bf16[6144,512]{1,0:T(8,128)(2,1)} %bitcast.6, bf16[512,512]{1,0:T(8,128)(2,1)} %solve_panel.1.solved_ref), custom_call_target="tpu_custom_call" | custom-call | tf_op jit(solution)/shard_map/products_sent/pallas_call | solution.py:138
  115.4 1.9 collective-permute-start
  117.3 4.3 %collective-permute-done.rest_0_ = bf16[4096,256]{1,0:T(8,128)(2,1)S(1)} collective-permute-done((bf16[4096,256]{1,0:T(8,128)(2,1)}, bf16[4096,256]{1,0:T(8,128)(2,1)S(1)}, u32[]{:S(2)}, u32[]{:S(2)}) %collective-permute-start) | collective-permute-done | bytes 2097184 | tf_op jit(solution)/shard_map/ppermute | solution.py:166
  121.6 0.0 copy-start
  121.6 1.3 copy-done
  123.0 10.4 %products_kept.1 = bf16[4096,256]{1,0:T(8,128)(2,1)} custom-call(s32[16]{0:T(128)} %get-tuple-element.6.table_ref, bf16[6144,512]{1,0:T(8,128)(2,1)} %bitcast.7, bf16[512,512]{1,0:T(8,128)(2,1)} %solve_panel.1.solved_ref, bf16[4096,256]{1,0:T(8,128)(2,1)} %copy-done), custom_call_target="tpu_custom_call" | custom-call | tf_op jit(solution)/shard_map/products_kept/pallas_call | solution.py:138
  133.4 63.6 %all_to_all.9 = bf16[16,256,256]{2,1,0:T(8,128)(2,1)S(1)} all-to-all(bf16[16,256,256]{2,1,0:T(8,128)(2,1)} %bitcast.8), channel_id=1, replica_groups=mesh['x_lo'=2,'y'=8,'core'=2,'x_hi'=2,'z'=12] {'x_lo','y'}, dimensions={0} | all-to-all | bytes 4194304 | tf_op jit(solution)/shard_map/all_to_all | solution.py:168
  197.0 0.0 copy-start.1
  197.0 0.3 convert_reduce_fusion
  197.3 0.7 copy-done.1
  197.9 0.7 sub.8
  (1 shorter events, 0.0 us)
Async XLA Ops:
  6.5 101.7 %all-gather.4.cloned.1.call-start = ((), (), s32[]{:S(2)}) async-start(), calls=%async_computation.1 | async-start | bytes 6815744 | tf_op jit(solution)/shard_map/all_gather | solution.py:151
  115.4 6.3 %collective-permute-start = (bf16[4096,256]{1,0:T(8,128)(2,1)}, bf16[4096,256]{1,0:T(8,128)(2,1)S(1)}, u32[]{:S(2)}, u32[]{:S(2)}) collective-permute-start(bf16[4096,256]{1,0:T(8,128)(2,1)} %products_sent.1), channel_id=1, source_target_pairs={{0,24},{24,0},{1,25},{25,1},{2,26},{26,2},{3,27},{27,3},{4,28},{28... | collective-permute-start | bytes 6291464 | tf_op jit(solution)/shard_map/ppermute | solution.py:166
  121.6 1.3 copy-start
  197.0 1.0 copy-start.1
Sparse Core Ops, SparseCore 0:
  17.2 90.9 all-gather.3

commit v2 on v1

--- a/solution.py
+++ b/solution.py
@@ -5,8 +5,11 @@
 from jax.experimental.pallas import tpu as pltpu
 from jax.sharding import Mesh, PartitionSpec as P
 
+
 BLOCK = 128
 GROUP = 8
+FIRST_ROWS = 160
+
 
 def invert_block(block):
     size = block.shape[0]
@@ -101,73 +104,78 @@
     )(diag, panel)
 
 
-def product_kernel(table_ref, tile_ref, solved_ref, *rest):
-    out_ref = rest[-1]
-    step = pl.program_id(0)
-    present = table_ref[step] >= 0
-    width = out_ref.shape[1]
+def product_kernel(table_ref, tiles_ref, solved_ref, sent_ref, kept_ref):
+    slots, _, width = sent_ref.shape
+    solved = solved_ref[...]
 
-    @pl.when(present)
-    def _():
-        both = jnp.dot(tile_ref[...], solved_ref[...], preferred_element_type=jnp.float32)
-        value = both[:, :width] + both[:, width:]
-        if len(rest) == 2:
-            value = value + rest[0][...].astype(jnp.float32)
-        out_ref[...] = value.astype(out_ref.dtype)
+    def place(slot, out_ref, row):
+        index = table_ref[row, slot]
 
-    @pl.when(jnp.logical_not(present))
-    def _():
-        if len(rest) == 2:
-            out_ref[...] = rest[0][...]
-        else:
-            out_ref[...] = jnp.zeros_like(out_ref)
+        @pl.when(index >= 0)
+        def _():
+            both = jnp.dot(tiles_ref[index], solved, preferred_element_type=jnp.float32)
+            out_ref[slot] = (both[:, :width] + both[:, width:]).astype(out_ref.dtype)
+
+        @pl.when(index < 0)
+        def _():
+            out_ref[slot] = jnp.zeros(out_ref.shape[1:], out_ref.dtype)
+
+    def step(slot, carry):
+        place(slot, sent_ref, 0)
+        place(slot, kept_ref, 1)
+        return carry
+
+    lax.fori_loop(0, slots, step, 0)
 
 
-def placed_products(table, tiles, solved, received, name):
-    slots, width = table.shape[0], tiles.shape[1]
-    tile = solved.shape[1] // 2
-    by_slot = pl.BlockSpec((tile, tile), lambda i, table: (i, 0))
-    in_specs = [
-        pl.BlockSpec((tile, width), lambda i, table: (jnp.maximum(table[i], 0), 0)),
-        pl.BlockSpec((width, 2 * tile), lambda i, table: (0, 0)),
-    ]
-    operands = [table, tiles, solved]
-    if received is not None:
-        in_specs.append(by_slot)
-        operands.append(received)
+def placed_products(table, tiles, solved):
+    half = jax.ShapeDtypeStruct(
+        (table.shape[1], tiles.shape[1], solved.shape[1] // 2), jnp.bfloat16
+    )
+    whole = pl.BlockSpec(memory_space=pltpu.VMEM)
     return pl.pallas_call(
         product_kernel,
-        grid_spec=pltpu.PrefetchScalarGridSpec(
-            num_scalar_prefetch=1, grid=(slots,), in_specs=in_specs, out_specs=by_slot
-        ),
-        out_shape=jax.ShapeDtypeStruct((slots * tile, tile), jnp.bfloat16),
-        name=name,
-    )(*operands)
+        in_specs=[pl.BlockSpec(memory_space=pltpu.SMEM), whole, whole],
+        out_specs=[whole, whole],
+        out_shape=[half, half],
+    )(table, tiles, solved)
 
 
 def local(diag_blocks, row_panel, col_panel, row_tiles, col_mask, slot_tile, trailing):
-    tile = trailing.shape[0]
-    pair = lax.all_gather(row_panel[0], "x_hi", axis=0, tiled=True)
-    tiles = lax.all_gather(pair, "z", axis=0, tiled=True)
-    solved = solve_panel(diag_blocks[0], col_panel[0])
-
+    width = row_panel.shape[2]
     count = row_tiles.shape[1]
     halves = lax.axis_size("x_hi")
+
+    first, second = row_panel[0, :FIRST_ROWS], row_panel[0, FIRST_ROWS:]
+    first = lax.all_gather(first, "x_hi", axis=0, tiled=True)
+    first, second = lax.optimization_barrier((first, second))
+    second = lax.all_gather(second, "x_hi", axis=0, tiled=True)
+    solved = solve_panel(diag_blocks[0], col_panel[0])
+    second, solved = lax.optimization_barrier((second, solved))
+    gathered = []
+    for pair in (first, second):
+        rows = lax.all_gather(pair, "z", axis=0, tiled=True)
+        gathered.append(rows.reshape(count, pair.shape[0] // halves, width))
+
     order = jnp.arange(count, dtype=jnp.int32)
     place = (order % (count // halves)) * halves + order // (count // halves)
     match = slot_tile[:, None] == row_tiles[0][None, :]
     table = jnp.max(jnp.where(match & (col_mask[0, 0] != 0), place[None, :], -1), axis=1)
-    table = table.reshape(-1, 2)
+    table = table.reshape(-1, 2).T
     core = lax.axis_index("core")
-    mine = jnp.where(core == 0, table[:, 0], table[:, 1])
-    other = jnp.where(core == 0, table[:, 1], table[:, 0])
+    table = jnp.where(core == 0, table[::-1], table)
 
-    sent = placed_products(other, tiles, solved, None, "products_sent")
-    received = lax.ppermute(sent, "core", [(0, 1), (1, 0)])
-    partial = placed_products(mine, tiles, solved, received, "products_kept")
-    pieces = lax.all_to_all(partial, ("x_lo", "y"), 0, 0, tiled=True)
-    pieces = pieces.reshape(-1, tile, tile).astype(jnp.float32)
-    return trailing - jnp.sum(pieces, axis=0)
+    stripes = []
+    for rows in gathered:
+        sent, kept = placed_products(table, rows, solved)
+        received = lax.ppermute(sent, "core", [(0, 1), (1, 0)])
+        partial = kept.astype(jnp.float32) + received.astype(jnp.float32)
+        partial = partial.astype(jnp.bfloat16)
+        if stripes:
+            partial, stripes[-1] = lax.optimization_barrier((partial, stripes[-1]))
+        pieces = lax.all_to_all(partial, ("x_lo", "y"), 0, 0, tiled=True)
+        stripes.append(jnp.sum(pieces.astype(jnp.float32), axis=0))
+    return trailing - jnp.concatenate(stripes, axis=0)
 
 
 def solution(mesh):
@@ -177,4 +185,5 @@
     )
     w, n = ("x_lo", "y", "core"), ("x_hi", "z")
     placed = (P(w), P(w, n), P(w, n), P(w), P(w, n), P(), P(w, n))
+
     return jax.shard_map(local, mesh=split, in_specs=placed, out_specs=P(w, n), check_vma=False)

time: 207 us -> 203 us (0.981)
  the two profiles are of different devices: /device:TPU:14 before, /device:TPU:12 now
where the time goes in v2:
time: 203 us; the launch traced here: 202 us
  waiting for transfers between devices  78.8 us (39%)
  blocking collectives  49.8 us (25%)
  Pallas kernels  33.8 us (17%)
  starting transfers between devices  18 us (9%)
  between operations  14.2 us (7%)
  other arithmetic  5.88 us (3%)
  local copies, waits for them, and re-layouts  2.04 us (1%)
    all_gather x2, waiting for transfers between devices, local(): rows = lax.all_gather(pair, 'z', axis=0, tiled=True)  73.5 us
    all_to_all x1, blocking collectives, local(): pieces = lax.all_to_all(partial, ('x_lo', 'y'), 0, 0, tiled=True)  34.7 us
    pallas_call x1, Pallas kernels, solve_panel(): pl.pallas_call(solve_kernel, out_shape=jax.ShapeDtypeStruct((width, 2 * t...  25.9 us
    all_to_all x1, starting transfers between devices, local(): pieces = lax.all_to_all(partial, ('x_lo', 'y'), 0, 0, tiled=True)  13.7 us
    all_gather x1, blocking collectives, local(): first = lax.all_gather(first, 'x_hi', axis=0, tiled=True)  8.21 us
    pallas_call x2, Pallas kernels, placed_products(): pl.pallas_call(product_kernel, in_specs=[pl.BlockSpec(memory_space=pltpu....  7.9 us
    all_gather x1, blocking collectives, local(): second = lax.all_gather(second, 'x_hi', axis=0, tiled=True)  6.88 us
    ppermute x2, waiting for transfers between devices, local(): received = lax.ppermute(sent, 'core', [(0, 1), (1, 0)])  5.31 us
  transfers between devices with their start and end apart: 5, of which 4 were waited for; matrix products, arithmetic and copies ran while one was open for 2% of the time, Pallas kernels for 17%

profile of v2, /device:TPU:12, one launch (start us, length us, event | category | flops | bytes accessed | tf_op | source)
XLA Modules:
  0.0 202.5 jit_solution(16751758112908310444)
XLA Ops:
  6.5 0.0 all-gather.6.cloned.1.call-start
  6.5 0.9 slice_bitcast_fusion
  7.4 0.9 slice.6
  8.4 0.0 copy-start.1
  8.4 0.0 copy-start.2
  8.4 8.2 %all-gather = bf16[1,320,512]{2,1,0:T(8,128)(2,1)} all-gather(bf16[1,160,512]{2,1,0:T(8,128)(2,1)S(1)} %slice.6), channel_id=2, replica_groups=mesh['x_lo'=2,'y'=8,'core'=2,'x_hi'=2,'z'=12] {'x_hi'}, dimensions={1}, use_global_device_ids=true | all-gather | bytes 491520 | tf_op jit(solution)/shard_map/all_gather | solution.py:150
  16.6 0.0 all-gather.6.cloned.1.call-update
  16.6 0.0 all-gather.4.cloned.1.call-start
  16.7 25.9 %solve_panel.1.solved_ref = bf16[512,512]{1,0:T(8,128)(2,1)} custom-call(f32[512,512]{1,0:T(8,128)} %bitcast.14, bf16[256,512]{1,0:T(8,128)(2,1)} %bitcast.15), custom_call_target="tpu_custom_call" | custom-call | tf_op jit(solution)/shard_map/solve_panel/pallas_call | solution.py:96
  42.6 6.9 %all_gather.13 = bf16[192,512]{1,0:T(8,128)(2,1)} all-gather(bf16[96,512]{1,0:T(8,128)(2,1)S(1)} %slice_bitcast_fusion), channel_id=1, replica_groups=mesh['x_lo'=2,'y'=8,'core'=2,'x_hi'=2,'z'=12] {'x_hi'}, dimensions={0}, use_global_device_ids=true | all-gather | bytes 294912 | tf_op jit(solution)/shard_map/all_gather | solution.py:152
  49.5 0.0 all-gather.4.cloned.1.call-update
  50.2 0.0 copy-done.1
  50.2 0.0 copy-done.2
  50.2 0.1 select_reduce_fusion
  50.3 0.1 reshape.31
  50.4 0.1 copy.10
  50.5 0.6 broadcast_select_fusion.table_ref
  51.0 37.9 %all-gather.6.cloned.1.call-done = bf16[3840,512]{1,0:T(8,128)(2,1)} async-done(((bf16[320,512]{1,0:T(8,128)(2,1)}), bf16[3840,512]{1,0:T(8,128)(2,1)}) %all-gather.6.cloned.1.call-update) | async-done | bytes 3932176 | tf_op jit(solution)/shard_map/all_gather | solution.py:157
  89.0 4.4 %shard_map.74 = (bf16[16,160,256]{2,1,0:T(8,128)(2,1)}, bf16[16,160,256]{2,1,0:T(8,128)(2,1)}) custom-call(s32[2,16]{1,0:T(2,128)} %broadcast_select_fusion.table_ref, bf16[24,160,512]{2,1,0:T(8,128)(2,1)} %bitcast.11, bf16[512,512]{1,0:T(8,128)(2,1)} %solve_panel.1.solved_ref), custom_call_target="tpu_custom_call" | custom-call | tf_op jit(solution)/shard_map/pallas_call | solution.py:136
  93.4 2.3 %collective-permute-start.1 = (bf16[16,160,256]{2,1,0:T(8,128)(2,1)}, bf16[16,160,256]{2,1,0:T(8,128)(2,1)S(1)}, u32[]{:S(2)}, u32[]{:S(2)}) collective-permute-start(bf16[16,160,256]{2,1,0:T(8,128)(2,1)} %get-tuple-element.22), channel_id=1, source_target_pairs={{0,24},{24,0},{1,25},{25,1},{2,26},{26,2},{3,27},{27,3},{4,28},{28... | collective-permute-start | bytes 3932168 | tf_op jit(solution)/shard_map/ppermute | solution.py:171
  95.7 2.9 %collective-permute-done.1 = bf16[16,160,256]{2,1,0:T(8,128)(2,1)S(1)} collective-permute-done((bf16[16,160,256]{2,1,0:T(8,128)(2,1)}, bf16[16,160,256]{2,1,0:T(8,128)(2,1)S(1)}, u32[]{:S(2)}, u32[]{:S(2)}) %collective-permute-start.1) | collective-permute-done | bytes 1310752 | tf_op jit(solution)/shard_map/ppermute | solution.py:171
  98.5 2.8 %add_convert_fusion = bf16[16,160,256]{2,1,0:T(8,128)(2,1)} fusion(bf16[16,160,256]{2,1,0:T(8,128)(2,1)S(1)} %collective-permute-done.1, bf16[16,160,256]{2,1,0:T(8,128)(2,1)} %get-tuple-element.21), kind=kLoop, calls=%fused_computation.1 | loop fusion | flops 2621440 | bytes 3932160 | tf_op jit(solution)/shard_map/convert_element_type | solution.py:173
  101.4 13.7 %all-to-all-start = ((bf16[16,160,256]{2,1,0:T(8,128)(2,1)}), bf16[16,160,256]{2,1,0:T(8,128)(2,1)S(1)}, u32[]{:S(2)}, u32[]{:S(2)}) async-start(bf16[16,160,256]{2,1,0:T(8,128)(2,1)} %add_convert_fusion), calls=%async_computation | async-start | bytes 2621440 | tf_op jit(solution)/shard_map/all_to_all | solution.py:176
  115.1 35.5 %all-gather.4.cloned.1.call-done = bf16[2304,512]{1,0:T(8,128)(2,1)} async-done(((bf16[192,512]{1,0:T(8,128)(2,1)}), bf16[2304,512]{1,0:T(8,128)(2,1)}) %all-gather.4.cloned.1.call-update) | async-done | bytes 2359312 | tf_op jit(solution)/shard_map/all_gather | solution.py:157
  150.7 3.5 %shard_map.73 = (bf16[16,96,256]{2,1,0:T(8,128)(2,1)}, bf16[16,96,256]{2,1,0:T(8,128)(2,1)}) custom-call(s32[2,16]{1,0:T(2,128)} %broadcast_select_fusion.table_ref, bf16[24,96,512]{2,1,0:T(8,128)(2,1)} %bitcast.12, bf16[512,512]{1,0:T(8,128)(2,1)} %solve_panel.1.solved_ref), custom_call_target="tpu_custom_call" | custom-call | tf_op jit(solution)/shard_map/pallas_call | solution.py:136
  154.2 1.9 collective-permute-start
  156.1 2.5 %collective-permute-done = bf16[16,96,256]{2,1,0:T(8,128)(2,1)S(1)} collective-permute-done((bf16[16,96,256]{2,1,0:T(8,128)(2,1)}, bf16[16,96,256]{2,1,0:T(8,128)(2,1)S(1)}, u32[]{:S(2)}, u32[]{:S(2)}) %collective-permute-start) | collective-permute-done | bytes 786464 | tf_op jit(solution)/shard_map/ppermute | solution.py:171
  158.5 1.4 add_convert_fusion.1
  159.9 0.0 all-to-all-done
  159.9 0.2 convert_reduce_fusion
  160.1 0.0 copy-start
  160.1 34.7 %all_to_all.10 = bf16[16,96,256]{2,1,0:T(8,128)(2,1)S(1)} all-to-all(bf16[16,96,256]{2,1,0:T(8,128)(2,1)S(1)} %add_convert_fusion.1), channel_id=1, replica_groups=mesh['x_lo'=2,'y'=8,'core'=2,'x_hi'=2,'z'=12] {'x_lo','y'}, dimensions={0} | all-to-all | bytes 1572864 | tf_op jit(solution)/shard_map/all_to_all | solution.py:176
  194.8 0.1 convert_reduce_fusion.1
  194.9 0.0 copy-done
  194.9 0.7 maximum_subtract_fusion
  (2 shorter events, 0.0 us)
Async XLA Ops:
  6.5 82.4 %all-gather.6.cloned.1.call-start = ((), (), s32[]{:S(2)}) async-start(), calls=%async_computation.3 | async-start | bytes 4259840 | tf_op jit(solution)/shard_map/all_gather | solution.py:157
  8.4 41.8 %copy-start.1 = (s32[32]{0:T(128)S(1)}, s32[32]{0:T(128)}, u32[]{:S(2)}) copy-start(s32[32]{0:T(128)} %param.12) | copy-start | bytes 388
  8.4 41.8 %copy-start.2 = (s32[1,24]{1,0:T(1,128)S(1)}, s32[1,24]{1,0:T(1,128)}, u32[]{:S(2)}) copy-start(s32[1,24]{1,0:T(1,128)} %param.10) | copy-start | bytes 292
  16.6 134.0 %all-gather.4.cloned.1.call-start = ((), (), s32[]{:S(2)}) async-start(), calls=%async_computation.2 | async-start | bytes 2555904 | tf_op jit(solution)/shard_map/all_gather | solution.py:157
  93.4 5.2 %collective-permute-start.1 = (bf16[16,160,256]{2,1,0:T(8,128)(2,1)}, bf16[16,160,256]{2,1,0:T(8,128)(2,1)S(1)}, u32[]{:S(2)}, u32[]{:S(2)}) collective-permute-start(bf16[16,160,256]{2,1,0:T(8,128)(2,1)} %get-tuple-element.22), channel_id=1, source_target_pairs={{0,24},{24,0},{1,25},{25,1},{2,26},{26,2},{3,27},{27,3},{4,28},{28... | collective-permute-start | bytes 3932168 | tf_op jit(solution)/shard_map/ppermute | solution.py:171
  101.4 58.5 %all-to-all-start = ((bf16[16,160,256]{2,1,0:T(8,128)(2,1)}), bf16[16,160,256]{2,1,0:T(8,128)(2,1)S(1)}, u32[]{:S(2)}, u32[]{:S(2)}) async-start(bf16[16,160,256]{2,1,0:T(8,128)(2,1)} %add_convert_fusion), calls=%async_computation | async-start | bytes 2621440 | tf_op jit(solution)/shard_map/all_to_all | solution.py:176
  154.2 4.4 %collective-permute-start = (bf16[16,96,256]{2,1,0:T(8,128)(2,1)}, bf16[16,96,256]{2,1,0:T(8,128)(2,1)S(1)}, u32[]{:S(2)}, u32[]{:S(2)}) collective-permute-start(bf16[16,96,256]{2,1,0:T(8,128)(2,1)} %get-tuple-element.19), channel_id=1, source_target_pairs={{0,24},{24,0},{1,25},{25,1},{2,26},{26,2},{3,27},{27,3},{4,28},{28... | collective-permute-start | bytes 2359304 | tf_op jit(solution)/shard_map/ppermute | solution.py:171
  160.1 34.8 %copy-start = (f32[256,256]{1,0:T(8,128)S(1)}, f32[256,256]{1,0:T(8,128)}, u32[]{:S(2)}) copy-start(f32[256,256]{1,0:T(8,128)} %param.13) | copy-start | bytes 786436
Sparse Core Ops, SparseCore 0:
  16.8 72.1 all-gather.5
  91.4 59.2 all-gather.3

commit v3 on v2

--- a/solution.py
+++ b/solution.py
@@ -8,7 +8,8 @@
 
 BLOCK = 128
 GROUP = 8
-FIRST_ROWS = 160
+FIRST_ROWS = 192
+TILES_PER_STEP = 6
 
 
 def invert_block(block):
@@ -104,41 +105,50 @@
     )(diag, panel)
 
 
-def product_kernel(table_ref, tiles_ref, solved_ref, sent_ref, kept_ref):
-    slots, _, width = sent_ref.shape
-    solved = solved_ref[...]
+def product_kernel(dest_ref, tiles_ref, solved_ref, sent_ref, kept_ref):
+    slots, rows, width = sent_ref.shape
+    tiles = tiles_ref.shape[0]
+    step = pl.program_id(0)
 
-    def place(slot, out_ref, row):
-        index = table_ref[row, slot]
+    @pl.when(step == 0)
+    def _():
+        sent_ref[...] = jnp.zeros(sent_ref.shape, sent_ref.dtype)
+        kept_ref[...] = jnp.zeros(kept_ref.shape, kept_ref.dtype)
 
-        @pl.when(index >= 0)
+    stacked = tiles_ref[...].reshape(tiles * rows, tiles_ref.shape[2])
+    both = jnp.dot(stacked, solved_ref[...], preferred_element_type=jnp.float32)
+    value = (both[:, :width] + both[:, width:]).astype(sent_ref.dtype)
+    for t in range(tiles):
+        dest = dest_ref[step * tiles + t]
+        part = value[t * rows : (t + 1) * rows]
+
+        @pl.when((dest >= 0) & (dest < slots))
         def _():
-            both = jnp.dot(tiles_ref[index], solved, preferred_element_type=jnp.float32)
-            out_ref[slot] = (both[:, :width] + both[:, width:]).astype(out_ref.dtype)
+            sent_ref[dest] = part
 
-        @pl.when(index < 0)
+        @pl.when(dest >= slots)
         def _():
-            out_ref[slot] = jnp.zeros(out_ref.shape[1:], out_ref.dtype)
-
-    def step(slot, carry):
-        place(slot, sent_ref, 0)
-        place(slot, kept_ref, 1)
-        return carry
-
-    lax.fori_loop(0, slots, step, 0)
+            kept_ref[dest - slots] = part
 
 
-def placed_products(table, tiles, solved):
-    half = jax.ShapeDtypeStruct(
-        (table.shape[1], tiles.shape[1], solved.shape[1] // 2), jnp.bfloat16
-    )
-    whole = pl.BlockSpec(memory_space=pltpu.VMEM)
+def placed_products(dest, tiles, solved, slots):
+    count, rows, width = tiles.shape
+    tile = solved.shape[1] // 2
+    half = jax.ShapeDtypeStruct((slots, rows, tile), jnp.bfloat16)
+    out = pl.BlockSpec((slots, rows, tile), lambda i, dest: (0, 0, 0))
     return pl.pallas_call(
         product_kernel,
-        in_specs=[pl.BlockSpec(memory_space=pltpu.SMEM), whole, whole],
-        out_specs=[whole, whole],
+        grid_spec=pltpu.PrefetchScalarGridSpec(
+            num_scalar_prefetch=1,
+            grid=(count // TILES_PER_STEP,),
+            in_specs=[
+                pl.BlockSpec((TILES_PER_STEP, rows, width), lambda i, dest: (i, 0, 0)),
+                pl.BlockSpec((width, 2 * tile), lambda i, dest: (0, 0)),
+            ],
+            out_specs=[out, out],
+        ),
         out_shape=[half, half],
-    )(table, tiles, solved)
+    )(dest, tiles, solved)
 
 
 def local(diag_blocks, row_panel, col_panel, row_tiles, col_mask, slot_tile, trailing):
@@ -146,10 +156,9 @@
     count = row_tiles.shape[1]
     halves = lax.axis_size("x_hi")
 
-    first, second = row_panel[0, :FIRST_ROWS], row_panel[0, FIRST_ROWS:]
-    first = lax.all_gather(first, "x_hi", axis=0, tiled=True)
-    first, second = lax.optimization_barrier((first, second))
-    second = lax.all_gather(second, "x_hi", axis=0, tiled=True)
+    first = lax.all_gather(row_panel[0, :FIRST_ROWS], "x_hi", axis=0, tiled=True)
+    first, rest = lax.optimization_barrier((first, row_panel))
+    second = lax.all_gather(rest[0, FIRST_ROWS:], "x_hi", axis=0, tiled=True)
     solved = solve_panel(diag_blocks[0], col_panel[0])
     second, solved = lax.optimization_barrier((second, solved))
     gathered = []
@@ -157,17 +166,17 @@
         rows = lax.all_gather(pair, "z", axis=0, tiled=True)
         gathered.append(rows.reshape(count, pair.shape[0] // halves, width))
 
-    order = jnp.arange(count, dtype=jnp.int32)
-    place = (order % (count // halves)) * halves + order // (count // halves)
-    match = slot_tile[:, None] == row_tiles[0][None, :]
-    table = jnp.max(jnp.where(match & (col_mask[0, 0] != 0), place[None, :], -1), axis=1)
-    table = table.reshape(-1, 2).T
-    core = lax.axis_index("core")
-    table = jnp.where(core == 0, table[::-1], table)
+    slots = slot_tile.shape[0] // 2
+    ids = row_tiles[0].reshape(halves, count // halves).T.reshape(count)
+    positions = jnp.arange(2 * slots, dtype=jnp.int32)
+    match = slot_tile[None, :] == ids[:, None]
+    kept_here = (positions % 2 == lax.axis_index("core")).astype(jnp.int32)
+    target = jnp.where(col_mask[0, 0] != 0, positions // 2 + slots * kept_here, -1)
+    dest = jnp.max(jnp.where(match, target[None, :], -1), axis=1)
 
     stripes = []
     for rows in gathered:
-        sent, kept = placed_products(table, rows, solved)
+        sent, kept = placed_products(dest, rows, solved, slots)
         received = lax.ppermute(sent, "core", [(0, 1), (1, 0)])
         partial = kept.astype(jnp.float32) + received.astype(jnp.float32)
         partial = partial.astype(jnp.bfloat16)

time: 203 us -> 204 us (level)
  the two profiles are of different devices: /device:TPU:12 before, /device:TPU:8 now
where the time goes in v3:
time: 204 us; the launch traced here: 203 us
  waiting for transfers between devices  89.6 us (44%)
  blocking collectives  39.2 us (19%)
  Pallas kernels  39.1 us (19%)
  between operations  14.1 us (7%)
  starting transfers between devices  11.9 us (6%)
  other arithmetic  7.29 us (4%)
    all_gather x2, waiting for transfers between devices, local(): rows = lax.all_gather(pair, 'z', axis=0, tiled=True)  83.9 us
    pallas_call x1, Pallas kernels, solve_panel(): pl.pallas_call(solve_kernel, out_shape=jax.ShapeDtypeStruct((width, 2 * t...  25.9 us
    all_to_all x1, blocking collectives, local(): pieces = lax.all_to_all(partial, ('x_lo', 'y'), 0, 0, tiled=True)  23.6 us
    pallas_call x2, Pallas kernels, placed_products(): pl.pallas_call(product_kernel, grid_spec=pltpu.PrefetchScalarGridSpec(num...  13.2 us
    all_gather x1, blocking collectives, local(): lax.all_gather(row_panel[0, :FIRST_ROWS], 'x_hi', axis=0, tiled=True)  9.05 us
    all_to_all x1, starting transfers between devices, local(): pieces = lax.all_to_all(partial, ('x_lo', 'y'), 0, 0, tiled=True)  8.07 us
    all_gather x1, blocking collectives, local(): second = lax.all_gather(rest[0, FIRST_ROWS:], 'x_hi', axis=0, tiled=True)  6.53 us
    ppermute x2, waiting for transfers between devices, local(): received = lax.ppermute(sent, 'core', [(0, 1), (1, 0)])  5.65 us
  transfers between devices with their start and end apart: 5, of which 4 were waited for; matrix products, arithmetic and copies ran while one was open for 3% of the time, Pallas kernels for 15%

profile of v3, /device:TPU:8, one launch (start us, length us, event | category | flops | bytes accessed | tf_op | source)
XLA Modules:
  0.0 202.9 jit_solution(1686208588566421771)
XLA Ops:
  6.5 0.0 all-gather.7.cloned.1.call-start
  6.5 0.9 slice.6
  7.5 0.0 slice-start
  7.5 0.0 copy-start.1
  7.5 9.0 %all-gather = bf16[1,384,512]{2,1,0:T(8,128)(2,1)} all-gather(bf16[1,192,512]{2,1,0:T(8,128)(2,1)S(1)} %slice.6), channel_id=2, replica_groups=mesh['x_lo'=2,'y'=8,'core'=2,'x_hi'=2,'z'=12] {'x_hi'}, dimensions={1}, use_global_device_ids=true | all-gather | bytes 589824 | tf_op jit(solution)/shard_map/all_gather | solution.py:159
  16.6 0.0 all-gather.7.cloned.1.call-update
  16.6 0.0 all-gather.5.cloned.1.call-start
  17.3 0.5 broadcast.75
  17.8 1.3 reduce.3
  19.1 0.1 reshape_squeeze.3
  19.2 0.1 copy.10
  19.3 0.1 eq.28
  19.4 25.9 %solve_panel.1.solved_ref = bf16[512,512]{1,0:T(8,128)(2,1)} custom-call(f32[512,512]{1,0:T(8,128)} %bitcast.11, bf16[256,512]{1,0:T(8,128)(2,1)} %bitcast.13), custom_call_target="tpu_custom_call" | custom-call | tf_op jit(solution)/shard_map/solve_panel/pallas_call | solution.py:97
  45.3 0.0 slice-done
  45.3 6.5 %all-gather.1 = bf16[1,128,512]{2,1,0:T(8,128)(2,1)} all-gather(bf16[1,64,512]{2,1,0:T(8,128)(2,1)S(1)} %slice-done), channel_id=3, replica_groups=mesh['x_lo'=2,'y'=8,'core'=2,'x_hi'=2,'z'=12] {'x_hi'}, dimensions={1}, use_global_device_ids=true | all-gather | bytes 196608 | tf_op jit(solution)/shard_map/all_gather | solution.py:161
  51.8 0.0 copy-done.1
  51.8 0.7 select_reduce_fusion.dest_ref
  52.5 40.2 %all-gather.7.cloned.1.call-done = bf16[4608,512]{1,0:T(8,128)(2,1)} async-done(((bf16[384,512]{1,0:T(8,128)(2,1)}), bf16[4608,512]{1,0:T(8,128)(2,1)}) %all-gather.7.cloned.1.call-update) | async-done | bytes 4718608 | tf_op jit(solution)/shard_map/all_gather | solution.py:166
  92.7 8.0 %shard_map.74 = (bf16[16,192,256]{2,1,0:T(8,128)(2,1)}, bf16[16,192,256]{2,1,0:T(8,128)(2,1)}) custom-call(s32[24]{0:T(128)} %select_reduce_fusion.dest_ref, bf16[24,192,512]{2,1,0:T(8,128)(2,1)} %bitcast.8, bf16[512,512]{1,0:T(8,128)(2,1)} %solve_panel.1.solved_ref), custom_call_target="tpu_custom_call" | custom-call | tf_op jit(solution)/shard_map/pallas_call | solution.py:139
  100.7 1.9 collective-permute-start.1
  102.6 0.0 all-gather.5.cloned.1.call-update
  102.6 3.6 %collective-permute-done.1 = bf16[16,192,256]{2,1,0:T(8,128)(2,1)S(1)} collective-permute-done((bf16[16,192,256]{2,1,0:T(8,128)(2,1)}, bf16[16,192,256]{2,1,0:T(8,128)(2,1)S(1)}, u32[]{:S(2)}, u32[]{:S(2)}) %collective-permute-start.1) | collective-permute-done | bytes 1572896 | tf_op jit(solution)/shard_map/ppermute | solution.py:180
  106.2 3.0 %add_convert_fusion = bf16[16,192,256]{2,1,0:T(8,128)(2,1)} fusion(bf16[16,192,256]{2,1,0:T(8,128)(2,1)S(1)} %collective-permute-done.1, bf16[16,192,256]{2,1,0:T(8,128)(2,1)} %get-tuple-element.21), kind=kLoop, calls=%fused_computation.1 | loop fusion | flops 3145728 | bytes 4718592 | tf_op jit(solution)/shard_map/convert_element_type | solution.py:182
  109.2 8.1 %all-to-all-start = ((bf16[16,192,256]{2,1,0:T(8,128)(2,1)}), bf16[16,192,256]{2,1,0:T(8,128)(2,1)S(1)}, u32[]{:S(2)}, u32[]{:S(2)}) async-start(bf16[16,192,256]{2,1,0:T(8,128)(2,1)} %add_convert_fusion), calls=%async_computation | async-start | bytes 3145728 | tf_op jit(solution)/shard_map/all_to_all | solution.py:185
  117.3 43.7 %all-gather.5.cloned.1.call-done = bf16[1536,512]{1,0:T(8,128)(2,1)} async-done(((bf16[128,512]{1,0:T(8,128)(2,1)}), bf16[1536,512]{1,0:T(8,128)(2,1)}) %all-gather.5.cloned.1.call-update) | async-done | bytes 1572880 | tf_op jit(solution)/shard_map/all_gather | solution.py:166
  161.0 5.3 %shard_map.73 = (bf16[16,64,256]{2,1,0:T(8,128)(2,1)}, bf16[16,64,256]{2,1,0:T(8,128)(2,1)}) custom-call(s32[24]{0:T(128)} %select_reduce_fusion.dest_ref, bf16[24,64,512]{2,1,0:T(8,128)(2,1)} %bitcast.9, bf16[512,512]{1,0:T(8,128)(2,1)} %solve_panel.1.solved_ref), custom_call_target="tpu_custom_call" | custom-call | tf_op jit(solution)/shard_map/pallas_call | solution.py:139
  166.2 1.9 collective-permute-start
  168.2 2.1 %collective-permute-done = bf16[16,64,256]{2,1,0:T(8,128)(2,1)S(1)} collective-permute-done((bf16[16,64,256]{2,1,0:T(8,128)(2,1)}, bf16[16,64,256]{2,1,0:T(8,128)(2,1)S(1)}, u32[]{:S(2)}, u32[]{:S(2)}) %collective-permute-start) | collective-permute-done | bytes 524320 | tf_op jit(solution)/shard_map/ppermute | solution.py:180
  170.2 1.2 add_convert_fusion.1
  171.4 0.0 copy-start
  171.5 0.0 all-to-all-done
  171.5 0.2 convert_reduce_fusion
  171.7 23.6 %all_to_all.10 = bf16[16,64,256]{2,1,0:T(8,128)(2,1)S(1)} all-to-all(bf16[16,64,256]{2,1,0:T(8,128)(2,1)S(1)} %add_convert_fusion.1), channel_id=1, replica_groups=mesh['x_lo'=2,'y'=8,'core'=2,'x_hi'=2,'z'=12] {'x_lo','y'}, dimensions={0} | all-to-all | bytes 1048576 | tf_op jit(solution)/shard_map/all_to_all | solution.py:185
  195.3 0.1 convert_reduce_fusion.1
  195.4 0.0 copy-done
  195.4 0.7 maximum_subtract_fusion
  (1 shorter events, 0.0 us)
Async XLA Ops:
  6.5 86.2 %all-gather.7.cloned.1.call-start = ((), (), s32[]{:S(2)}) async-start(), calls=%async_computation.3 | async-start | bytes 5111808 | tf_op jit(solution)/shard_map/all_gather | solution.py:166
  7.5 37.8 %slice-start = ((bf16[1,256,512]{2,1,0:T(8,128)(2,1)}), bf16[1,64,512]{2,1,0:T(8,128)(2,1)S(1)}, s32[]{:S(2)}) async-start(bf16[1,256,512]{2,1,0:T(8,128)(2,1)} %param.8), calls=%async_computation.4 | async-start | bytes 131072 | tf_op jit(solution)/shard_map/slice | solution.py:161
  7.5 44.3 %copy-start.1 = (s32[32]{0:T(128)S(1)}, s32[32]{0:T(128)}, u32[]{:S(2)}) copy-start(s32[32]{0:T(128)} %param.12) | copy-start | bytes 388
  16.6 144.4 %all-gather.5.cloned.1.call-start = ((), (), s32[]{:S(2)}) async-start(), calls=%async_computation.2 | async-start | bytes 1703936 | tf_op jit(solution)/shard_map/all_gather | solution.py:166
  100.7 5.5 %collective-permute-start.1 = (bf16[16,192,256]{2,1,0:T(8,128)(2,1)}, bf16[16,192,256]{2,1,0:T(8,128)(2,1)S(1)}, u32[]{:S(2)}, u32[]{:S(2)}) collective-permute-start(bf16[16,192,256]{2,1,0:T(8,128)(2,1)} %get-tuple-element.22), channel_id=1, source_target_pairs={{0,24},{24,0},{1,25},{25,1},{2,26},{26,2},{3,27},{27,3},{4,28},{28... | collective-permute-start | bytes 4718600 | tf_op jit(solution)/shard_map/ppermute | solution.py:180
  109.2 62.2 %all-to-all-start = ((bf16[16,192,256]{2,1,0:T(8,128)(2,1)}), bf16[16,192,256]{2,1,0:T(8,128)(2,1)S(1)}, u32[]{:S(2)}, u32[]{:S(2)}) async-start(bf16[16,192,256]{2,1,0:T(8,128)(2,1)} %add_convert_fusion), calls=%async_computation | async-start | bytes 3145728 | tf_op jit(solution)/shard_map/all_to_all | solution.py:185
  166.2 4.0 %collective-permute-start = (bf16[16,64,256]{2,1,0:T(8,128)(2,1)}, bf16[16,64,256]{2,1,0:T(8,128)(2,1)S(1)}, u32[]{:S(2)}, u32[]{:S(2)}) collective-permute-start(bf16[16,64,256]{2,1,0:T(8,128)(2,1)} %get-tuple-element.19), channel_id=1, source_target_pairs={{0,24},{24,0},{1,25},{25,1},{2,26},{26,2},{3,27},{27,3},{4,28},{28... | collective-permute-start | bytes 1572872 | tf_op jit(solution)/shard_map/ppermute | solution.py:180
  171.4 23.9 %copy-start = (f32[256,256]{1,0:T(8,128)S(1)}, f32[256,256]{1,0:T(8,128)}, u32[]{:S(2)}) copy-start(f32[256,256]{1,0:T(8,128)} %param.13) | copy-start | bytes 786436
Sparse Core Ops, SparseCore 0:
  16.7 75.9 all-gather.6
  102.8 58.1 all-gather.4

commit v4 on v3

--- a/solution.py
+++ b/solution.py
@@ -8,7 +8,8 @@
 
 BLOCK = 128
 GROUP = 8
-FIRST_ROWS = 192
+FIRST_ROWS = 128
+SYNC_ROWS = 32
 TILES_PER_STEP = 6
 
 
@@ -105,9 +106,9 @@
     )(diag, panel)
 
 
-def product_kernel(dest_ref, tiles_ref, solved_ref, sent_ref, kept_ref):
-    slots, rows, width = sent_ref.shape
-    tiles = tiles_ref.shape[0]
+def product_kernel(dest_ref, *refs):
+    *tile_refs, solved_ref, sent_ref, kept_ref = refs
+    slots, _, width = sent_ref.shape
     step = pl.program_id(0)
 
     @pl.when(step == 0)
@@ -115,40 +116,49 @@
         sent_ref[...] = jnp.zeros(sent_ref.shape, sent_ref.dtype)
         kept_ref[...] = jnp.zeros(kept_ref.shape, kept_ref.dtype)
 
-    stacked = tiles_ref[...].reshape(tiles * rows, tiles_ref.shape[2])
-    both = jnp.dot(stacked, solved_ref[...], preferred_element_type=jnp.float32)
-    value = (both[:, :width] + both[:, width:]).astype(sent_ref.dtype)
-    for t in range(tiles):
-        dest = dest_ref[step * tiles + t]
-        part = value[t * rows : (t + 1) * rows]
-
-        @pl.when((dest >= 0) & (dest < slots))
-        def _():
-            sent_ref[dest] = part
-
-        @pl.when(dest >= slots)
-        def _():
-            kept_ref[dest - slots] = part
-
-
-def placed_products(dest, tiles, solved, slots):
-    count, rows, width = tiles.shape
+    low = 0
+    for tiles_ref in tile_refs:
+        tiles, rows, depth = tiles_ref.shape
+        stacked = tiles_ref[...].reshape(tiles * rows, depth)
+        both = jnp.dot(stacked, solved_ref[...], preferred_element_type=jnp.float32)
+        value = (both[:, :width] + both[:, width:]).astype(sent_ref.dtype)
+        high = low + rows
+        for t in range(tiles):
+            dest = dest_ref[step * tiles + t]
+            part = value[t * rows : (t + 1) * rows]
+
+            @pl.when((dest >= 0) & (dest < slots))
+            def _():
+                sent_ref[dest, low:high] = part
+
+            @pl.when(dest >= slots)
+            def _():
+                kept_ref[dest - slots, low:high] = part
+
+        low = high
+
+
+def placed_products(dest, groups, solved, slots):
+    count, _, width = groups[0].shape
+    rows = sum(group.shape[1] for group in groups)
     tile = solved.shape[1] // 2
     half = jax.ShapeDtypeStruct((slots, rows, tile), jnp.bfloat16)
     out = pl.BlockSpec((slots, rows, tile), lambda i, dest: (0, 0, 0))
+    in_specs = [
+        pl.BlockSpec((TILES_PER_STEP, group.shape[1], width), lambda i, dest: (i, 0, 0))
+        for group in groups
+    ]
+    in_specs.append(pl.BlockSpec((width, 2 * tile), lambda i, dest: (0, 0)))
     return pl.pallas_call(
         product_kernel,
         grid_spec=pltpu.PrefetchScalarGridSpec(
             num_scalar_prefetch=1,
             grid=(count // TILES_PER_STEP,),
-            in_specs=[
-                pl.BlockSpec((TILES_PER_STEP, rows, width), lambda i, dest: (i, 0, 0)),
-                pl.BlockSpec((width, 2 * tile), lambda i, dest: (0, 0)),
-            ],
+            in_specs=in_specs,
             out_specs=[out, out],
         ),
         out_shape=[half, half],
-    )(dest, tiles, solved)
+    )(dest, *groups, solved)
 
 
 def local(diag_blocks, row_panel, col_panel, row_tiles, col_mask, slot_tile, trailing):
@@ -156,15 +166,21 @@
     count = row_tiles.shape[1]
     halves = lax.axis_size("x_hi")
 
-    first = lax.all_gather(row_panel[0, :FIRST_ROWS], "x_hi", axis=0, tiled=True)
+    def over_x(rows):
+        return lax.all_gather(rows, "x_hi", axis=0)
+
+    def over_z(pair):
+        rows = lax.all_gather(pair.reshape(-1, width), "z", axis=0, tiled=True)
+        return rows.reshape(count, pair.shape[1], width)
+
+    first = over_x(row_panel[0, :FIRST_ROWS])
     first, rest = lax.optimization_barrier((first, row_panel))
-    second = lax.all_gather(rest[0, FIRST_ROWS:], "x_hi", axis=0, tiled=True)
+    rest = over_x(rest[0, FIRST_ROWS:])
+    early = over_z(first)
+    middle, late = rest[:, :SYNC_ROWS], over_z(rest[:, SYNC_ROWS:])
     solved = solve_panel(diag_blocks[0], col_panel[0])
-    second, solved = lax.optimization_barrier((second, solved))
-    gathered = []
-    for pair in (first, second):
-        rows = lax.all_gather(pair, "z", axis=0, tiled=True)
-        gathered.append(rows.reshape(count, pair.shape[0] // halves, width))
+    middle, solved = lax.optimization_barrier((middle, solved))
+    gathered = ((early, over_z(middle)), (late,))
 
     slots = slot_tile.shape[0] // 2
     ids = row_tiles[0].reshape(halves, count // halves).T.reshape(count)
@@ -175,8 +191,8 @@
     dest = jnp.max(jnp.where(match, target[None, :], -1), axis=1)
 
     stripes = []
-    for rows in gathered:
-        sent, kept = placed_products(dest, rows, solved, slots)
+    for groups in gathered:
+        sent, kept = placed_products(dest, groups, solved, slots)
         received = lax.ppermute(sent, "core", [(0, 1), (1, 0)])
         partial = kept.astype(jnp.float32) + received.astype(jnp.float32)
         partial = partial.astype(jnp.bfloat16)

time: 204 us -> 200 us (0.980)
  waiting for transfers between devices: 89.6 us -> 35.3 us
  blocking collectives: 39.2 us -> 88.3 us
    all_gather x2, waiting for transfers between devices: 83.9 us -> 29.6 us  [over_z(): rows = lax.all_gather(pair.reshape(-1, width), 'z', axis=0, tiled=True)]
    all_gather x2 -> x3, blocking collectives: 15.6 us -> 58.4 us  [the longest x1 43.7 us: over_z(): rows = lax.all_gather(pair.reshape(-1, width), 'z', axis=0, tiled=True)]
    all_to_all x1, blocking collectives: 23.6 us -> 29.9 us  [local(): pieces = lax.all_to_all(partial, ('x_lo', 'y'), 0, 0, tiled=True)]
  transfers between devices with their start and end apart: 5 -> 5, of which waited for: 4 -> 3; matrix products, arithmetic and copies ran while one was open for 3% -> 4% of each run, Pallas kernels for 15% -> 20%
where the time goes in v4:
time: 200 us
  blocking collectives  88.3 us (44%)
  Pallas kernels  40.3 us (20%)
  waiting for transfers between devices  35.3 us (18%)
  between operations  14.2 us (7%)
  starting transfers between devices  11.6 us (6%)
  other arithmetic  6.58 us (3%)
  local copies, waits for them, and re-layouts  3.39 us (2%)
    all_gather x1, blocking collectives, over_z(): rows = lax.all_gather(pair.reshape(-1, width), 'z', axis=0, tiled=True)  43.7 us
    all_to_all x1, blocking collectives, local(): pieces = lax.all_to_all(partial, ('x_lo', 'y'), 0, 0, tiled=True)  29.9 us
    all_gather x2, waiting for transfers between devices, over_z(): rows = lax.all_gather(pair.reshape(-1, width), 'z', axis=0, tiled=True)  29.6 us
    pallas_call x1, Pallas kernels, solve_panel(): pl.pallas_call(solve_kernel, out_shape=jax.ShapeDtypeStruct((width, 2 * t...  25.9 us
    all_gather x2, blocking collectives, over_x(): return lax.all_gather(rows, 'x_hi', axis=0)  14.7 us
    pallas_call x2, Pallas kernels, placed_products(): pl.pallas_call(product_kernel, grid_spec=pltpu.PrefetchScalarGridSpec(num...  14.4 us
    all_to_all x1, starting transfers between devices, local(): pieces = lax.all_to_all(partial, ('x_lo', 'y'), 0, 0, tiled=True)  7.7 us
    ppermute x2, waiting for transfers between devices, local(): received = lax.ppermute(sent, 'core', [(0, 1), (1, 0)])  5.67 us
  transfers between devices with their start and end apart: 5, of which 3 were waited for; matrix products, arithmetic and copies ran while one was open for 4% of the time, Pallas kernels for 20%

profile of v4, /device:TPU:8, one launch (start us, length us, event | category | flops | bytes accessed | tf_op | source)
XLA Modules:
  0.0 199.6 jit_solution(16220406895895163339)
XLA Ops:
  6.5 0.0 all-gather.5.cloned.1.call-start
  6.5 0.9 slice.12
  7.5 7.5 %all_gather.15 = bf16[2,128,512]{2,1,0:T(8,128)(2,1)} all-gather(bf16[1,128,512]{2,1,0:T(8,128)(2,1)S(1)} %slice.12), channel_id=1, replica_groups=mesh['x_lo'=2,'y'=8,'core'=2,'x_hi'=2,'z'=12] {'x_hi'}, dimensions={0}, use_global_device_ids=true | all-gather | bytes 393216 | tf_op jit(solution)/shard_map/all_gather | solution.py:170
  15.0 0.0 all-gather.5.cloned.1.call-update
  15.0 0.0 copy-start.2
  15.0 0.0 copy-start.1
  15.0 0.0 all-gather.3.cloned.1.call-start
  15.1 0.9 slice.13
  16.0 7.1 %all_gather.16 = bf16[2,128,512]{2,1,0:T(8,128)(2,1)S(1)} all-gather(bf16[1,128,512]{2,1,0:T(8,128)(2,1)S(1)} %slice.13), channel_id=1, replica_groups=mesh['x_lo'=2,'y'=8,'core'=2,'x_hi'=2,'z'=12] {'x_hi'}, dimensions={0}, use_global_device_ids=true | all-gather | bytes 393216 | tf_op jit(solution)/shard_map/all_gather | solution.py:170
  23.1 0.7 slice.16
  23.8 0.0 all-gather.3.cloned.1.call-update
  23.9 25.9 %solve_panel.1.refs_1_.refs_2_ = bf16[512,512]{1,0:T(8,128)(2,1)} custom-call(f32[512,512]{1,0:T(8,128)} %bitcast.13, bf16[256,512]{1,0:T(8,128)(2,1)} %bitcast.16), custom_call_target="tpu_custom_call" | custom-call | tf_op jit(solution)/shard_map/solve_panel/pallas_call | solution.py:98
  49.8 0.6 broadcast.75
  50.3 0.0 copy-done.2
  50.3 0.7 reduce.3
  51.0 0.1 reshape_squeeze.3
  51.1 0.1 copy.11
  51.2 0.1 eq.28
  51.9 0.0 copy-done.1
  51.9 0.7 select_reduce_fusion.dest_ref
  52.7 43.7 %all_gather.19 = bf16[768,512]{1,0:T(8,128)(2,1)} all-gather(bf16[64,512]{1,0:T(8,128)(2,1)S(1)} %bitcast.17), channel_id=1, replica_groups=mesh['x_lo'=2,'y'=8,'core'=2,'x_hi'=2,'z'=12] {'z'}, dimensions={0}, use_global_device_ids=true | all-gather | bytes 851968 | tf_op jit(solution)/shard_map/all_gather | solution.py:173
  96.4 0.0 all-gather.5.cloned.1.call-done
  96.4 8.4 %shard_map.74 = (bf16[16,160,256]{2,1,0:T(8,128)(2,1)}, bf16[16,160,256]{2,1,0:T(8,128)(2,1)}) custom-call(s32[24]{0:T(128)} %select_reduce_fusion.dest_ref, bf16[24,128,512]{2,1,0:T(8,128)(2,1)} %bitcast.10, bf16[24,32,512]{2,1,0:T(8,128)(2,1)} %bitcast.11, bf16[512,512]{1,0:T(8,128)(2,1)} %solve_panel.1.refs_1_.refs_2_), custom_call_target="tpu_custom_call" | custom-call | tf_op jit(solution)/shard_map/pallas_call | solution.py:152
  104.9 1.9 collective-permute-start.1
  106.8 3.2 %collective-permute-done.1 = bf16[16,160,256]{2,1,0:T(8,128)(2,1)S(1)} collective-permute-done((bf16[16,160,256]{2,1,0:T(8,128)(2,1)}, bf16[16,160,256]{2,1,0:T(8,128)(2,1)S(1)}, u32[]{:S(2)}, u32[]{:S(2)}) %collective-permute-start.1) | collective-permute-done | bytes 1310752 | tf_op jit(solution)/shard_map/ppermute | solution.py:196
  110.0 2.8 %add_convert_fusion = bf16[16,160,256]{2,1,0:T(8,128)(2,1)} fusion(bf16[16,160,256]{2,1,0:T(8,128)(2,1)S(1)} %collective-permute-done.1, bf16[16,160,256]{2,1,0:T(8,128)(2,1)} %get-tuple-element.21), kind=kLoop, calls=%fused_computation.1 | loop fusion | flops 2621440 | bytes 3932160 | tf_op jit(solution)/shard_map/convert_element_type | solution.py:198
  112.8 7.7 %all-to-all-start = ((bf16[16,160,256]{2,1,0:T(8,128)(2,1)}), bf16[16,160,256]{2,1,0:T(8,128)(2,1)S(1)}, u32[]{:S(2)}, u32[]{:S(2)}) async-start(bf16[16,160,256]{2,1,0:T(8,128)(2,1)} %add_convert_fusion), calls=%async_computation | async-start | bytes 2621440 | tf_op jit(solution)/shard_map/all_to_all | solution.py:201
  120.5 29.6 %all-gather.3.cloned.1.call-done = bf16[2304,512]{1,0:T(8,128)(2,1)} async-done(((bf16[192,512]{1,0:T(8,128)(2,1)}), bf16[2304,512]{1,0:T(8,128)(2,1)}) %all-gather.3.cloned.1.call-update) | async-done | bytes 2359312 | tf_op jit(solution)/shard_map/all_gather | solution.py:173
  150.1 5.9 %shard_map.73 = (bf16[16,96,256]{2,1,0:T(8,128)(2,1)}, bf16[16,96,256]{2,1,0:T(8,128)(2,1)}) custom-call(s32[24]{0:T(128)} %select_reduce_fusion.dest_ref, bf16[24,96,512]{2,1,0:T(8,128)(2,1)} %bitcast.12, bf16[512,512]{1,0:T(8,128)(2,1)} %solve_panel.1.refs_1_.refs_2_), custom_call_target="tpu_custom_call" | custom-call | tf_op jit(solution)/shard_map/pallas_call | solution.py:152
  156.0 1.9 collective-permute-start
  157.9 2.5 %collective-permute-done = bf16[16,96,256]{2,1,0:T(8,128)(2,1)S(1)} collective-permute-done((bf16[16,96,256]{2,1,0:T(8,128)(2,1)}, bf16[16,96,256]{2,1,0:T(8,128)(2,1)S(1)}, u32[]{:S(2)}, u32[]{:S(2)}) %collective-permute-start) | collective-permute-done | bytes 786464 | tf_op jit(solution)/shard_map/ppermute | solution.py:196
  160.4 1.4 add_convert_fusion.1
  161.7 0.0 all-to-all-done
  161.8 0.2 convert_reduce_fusion
  161.9 0.0 copy-start
  161.9 29.9 %all_to_all.10 = bf16[16,96,256]{2,1,0:T(8,128)(2,1)S(1)} all-to-all(bf16[16,96,256]{2,1,0:T(8,128)(2,1)S(1)} %add_convert_fusion.1), channel_id=1, replica_groups=mesh['x_lo'=2,'y'=8,'core'=2,'x_hi'=2,'z'=12] {'x_lo','y'}, dimensions={0} | all-to-all | bytes 1572864 | tf_op jit(solution)/shard_map/all_to_all | solution.py:201
  191.9 0.1 convert_reduce_fusion.1
  192.0 0.0 copy-done
  192.0 0.7 maximum_subtract_fusion
  (2 shorter events, 0.0 us)
Async XLA Ops:
  6.5 89.9 %all-gather.5.cloned.1.call-start = ((), (), s32[]{:S(2)}) async-start(), calls=%async_computation.3 | async-start | bytes 3407872 | tf_op jit(solution)/shard_map/all_gather | solution.py:173
  15.0 35.4 %copy-start.2 = (s32[1,24]{1,0:T(1,128)S(1)}, s32[1,24]{1,0:T(1,128)}, u32[]{:S(2)}) copy-start(s32[1,24]{1,0:T(1,128)} %param.10) | copy-start | bytes 292
  15.0 36.9 %copy-start.1 = (s32[32]{0:T(128)S(1)}, s32[32]{0:T(128)}, u32[]{:S(2)}) copy-start(s32[32]{0:T(128)} %param.12) | copy-start | bytes 388
  15.0 135.0 %all-gather.3.cloned.1.call-start = ((), (), s32[]{:S(2)}) async-start(), calls=%async_computation.2 | async-start | bytes 2555904 | tf_op jit(solution)/shard_map/all_gather | solution.py:173
  104.9 5.1 %collective-permute-start.1 = (bf16[16,160,256]{2,1,0:T(8,128)(2,1)}, bf16[16,160,256]{2,1,0:T(8,128)(2,1)S(1)}, u32[]{:S(2)}, u32[]{:S(2)}) collective-permute-start(bf16[16,160,256]{2,1,0:T(8,128)(2,1)} %get-tuple-element.22), channel_id=1, source_target_pairs={{0,24},{24,0},{1,25},{25,1},{2,26},{26,2},{3,27},{27,3},{4,28},{28... | collective-permute-start | bytes 3932168 | tf_op jit(solution)/shard_map/ppermute | solution.py:196
  112.8 49.0 %all-to-all-start = ((bf16[16,160,256]{2,1,0:T(8,128)(2,1)}), bf16[16,160,256]{2,1,0:T(8,128)(2,1)S(1)}, u32[]{:S(2)}, u32[]{:S(2)}) async-start(bf16[16,160,256]{2,1,0:T(8,128)(2,1)} %add_convert_fusion), calls=%async_computation | async-start | bytes 2621440 | tf_op jit(solution)/shard_map/all_to_all | solution.py:201
  156.0 4.4 %collective-permute-start = (bf16[16,96,256]{2,1,0:T(8,128)(2,1)}, bf16[16,96,256]{2,1,0:T(8,128)(2,1)S(1)}, u32[]{:S(2)}, u32[]{:S(2)}) collective-permute-start(bf16[16,96,256]{2,1,0:T(8,128)(2,1)} %get-tuple-element.18), channel_id=1, source_target_pairs={{0,24},{24,0},{1,25},{25,1},{2,26},{26,2},{3,27},{27,3},{4,28},{28... | collective-permute-start | bytes 2359304 | tf_op jit(solution)/shard_map/ppermute | solution.py:196
  161.9 30.1 %copy-start = (f32[256,256]{1,0:T(8,128)S(1)}, f32[256,256]{1,0:T(8,128)}, u32[]{:S(2)}) copy-start(f32[256,256]{1,0:T(8,128)} %param.13) | copy-start | bytes 786436
Sparse Core Ops, SparseCore 0:
  15.1 73.7 all-gather.4
  91.3 58.7 all-gather.2
